TPU v7x, 128 devices: a whole 4x4x4 slice. The times are simulated.
128 devices in a mesh: front: 8 (over z_hi, x), row: 8 (over y, core), col: 2 (over z_lo).
Axes of the slice: x: 4, y: 4, z: 4 (z_hi: 2, z_lo: 2; z = z_hi * 2 + z_lo), core: 2. Of those that a mesh axis runs over, the one named last changes fastest.
Arguments:
- pivot_block: float32 [16, 512, 512], P(('front', 'col'), 'row'), as said below
- panel_rows: float32 [16, 4096, 512], P(('front', 'col'), 'row'), may hold values from -0.875 to 0.875
- update_block: float32 [16, 4096, 4096], P(('front', 'col'), 'row'), as said below
- tile_map: int32 [16, 32], replicated, may hold values from 0 to 95, as said below
Outputs:
- pivot_factor: float32 [16, 512, 512], P(('front', 'col'), 'row')
- panel_factor: float32 [16, 4096, 512], P(('front', 'col'), 'row')
- parent_update: float32 [2, 12288, 12288], P('col', 'front', 'row')
Inputs may be any that keep to these rules, and one draw needn't show every extreme that they name: `pivot_block`: each child's pivot block is symmetric positive definite. `update_block`: each child's update block is symmetric. `tile_map`: row c lists, strictly increasing, the parent tiles that receive child c's 32 tiles; child c belongs to parent c % 2. At most 5 entries of one row fall in any aligned block of 12 parent tiles, and exactly 5 do in some block.
All inputs are finite; a program needn't handle non-finite values.
Results may differ from a plain program's by a relative error of at most 0.0001.
Values sent between devices are 32-bit elements; how exact they have to be, the bound alone decides.
No kernel may reach another device: no remote copies, remote signals or barrier semaphores. Data moves between devices by JAX's collectives and lax.ppermute only.
A program may use at most 192 MiB of HBM per device.

v0:
```python
import jax
import jax.numpy as jnp
from jax import lax
from jax.sharding import PartitionSpec as P

TILE = 128
PARENT = 12288


def solve_panel(lower_factor, panel_block):
    return jax.scipy.linalg.solve_triangular(lower_factor, panel_block.T, lower=True).T


def block_slots(tile_ids, block_count, block_width, slot_count):
    owners = tile_ids // block_width
    block_ids = jnp.arange(block_count, dtype=jnp.int32)
    starts = jnp.sum((owners[None, :] < block_ids[:, None]).astype(jnp.int32), axis=1)
    counts = jnp.sum((owners[None, :] == block_ids[:, None]).astype(jnp.int32), axis=1)
    slot_ids = jnp.arange(slot_count, dtype=jnp.int32)
    picks = jnp.minimum(starts[:, None] + slot_ids[None, :], tile_ids.shape[0] - 1)
    usable = slot_ids[None, :] < counts[:, None]
    return (picks, usable)


def local_onehot(child_maps, block_me, block_width, slot_count):
    owners = child_maps // block_width
    starts = jnp.sum((owners < block_me).astype(jnp.int32), axis=1)
    counts = jnp.sum((owners == block_me).astype(jnp.int32), axis=1)
    slot_ids = jnp.arange(slot_count, dtype=jnp.int32)
    picks = jnp.minimum(starts[:, None] + slot_ids[None, :], child_maps.shape[1] - 1)
    local_tile = jnp.take_along_axis(child_maps, picks, axis=1) - block_me * block_width
    usable = slot_ids[None, :] < counts[:, None]
    targets = jnp.arange(block_width, dtype=jnp.int32)
    onehot = (local_tile[:, None, :] == targets[None, :, None]) & usable[:, None, :]
    return onehot.astype(jnp.float32)


def local(pivot_block, panel_rows, update_block, tile_map):
    row_count = lax.axis_size("row")
    front_count = lax.axis_size("front")
    col_count = lax.axis_size("col")
    row_me = lax.axis_index("row")
    front_me = lax.axis_index("front")
    col_me = lax.axis_index("col")
    tile_size = TILE
    pivot_share = pivot_block.shape[1]
    own_rows = panel_rows.shape[1]
    contrib_order = update_block.shape[2]
    tile_count = contrib_order // tile_size
    block_width = PARENT // tile_size // row_count
    slot_count = tile_count // row_count + 1
    child_index = front_me * col_count + col_me
    tile_ids = lax.dynamic_index_in_dim(tile_map, child_index, 0, keepdims=False)
    pivot_whole = lax.all_gather(pivot_block[0], "row", axis=0, tiled=True)
    lower_factor = jnp.linalg.cholesky(pivot_whole)
    own_factor = solve_panel(lower_factor, panel_rows[0])
    all_factor = lax.all_gather(own_factor, "row", axis=0, tiled=True)
    col_picks, col_usable = block_slots(tile_ids, row_count, block_width, slot_count)
    contribution = update_block[0] - jnp.dot(
        own_factor, all_factor.T, precision=lax.Precision.HIGHEST
    )
    shaped = contribution.reshape(own_rows, tile_count, tile_size)
    picked = jnp.take(shaped, col_picks.reshape(-1), axis=1)
    picked = picked.reshape(own_rows, row_count, slot_count, tile_size)
    source = jnp.where(col_usable[None, :, :, None], picked, 0.0)
    arrived = lax.all_to_all(source, "row", split_axis=1, concat_axis=0, tiled=True)
    arrived = arrived.reshape(contrib_order, slot_count, tile_size)
    row_picks, row_usable = block_slots(tile_ids, front_count, block_width, slot_count)
    shaped = arrived.reshape(tile_count, tile_size, slot_count, tile_size)
    picked = jnp.take(shaped, row_picks.reshape(-1), axis=0)
    picked = picked.reshape(front_count, slot_count, tile_size, slot_count, tile_size)
    picked = jnp.where(row_usable[:, :, None, None, None], picked, 0.0)
    routed = lax.all_to_all(picked, "front", split_axis=0, concat_axis=0, tiled=True)
    sources = jnp.arange(front_count, dtype=jnp.int32) * col_count + col_me
    child_maps = jnp.take(tile_map, sources, axis=0)
    row_hot = local_onehot(child_maps, front_me, block_width, slot_count)
    col_hot = local_onehot(child_maps, row_me, block_width, slot_count)
    partial_value = jnp.einsum("fsxty,fbt->fsxby", routed, col_hot, precision=lax.Precision.HIGHEST)
    parent = jnp.einsum("fas,fsxby->axby", row_hot, partial_value, precision=lax.Precision.HIGHEST)
    parent = parent.reshape(block_width * tile_size, block_width * tile_size)
    pivot_rows_out = lax.dynamic_slice_in_dim(lower_factor, row_me * pivot_share, pivot_share, 0)
    return (pivot_rows_out[None], own_factor[None], parent[None])


def solution(mesh):
    return jax.shard_map(
        local,
        mesh=mesh,
        in_specs=(
            P(("front", "col"), "row", None),
            P(("front", "col"), "row", None),
            P(("front", "col"), "row", None),
            P(),
        ),
        out_specs=(
            P(("front", "col"), "row", None),
            P(("front", "col"), "row", None),
            P("col", "front", "row"),
        ),
        check_vma=False,
    )
```

profile of v0, /device:TPU:6, one launch (start us, length us, event | category | flops | bytes accessed | tf_op | source)
XLA Modules:
  0.0 728.1 jit_solution(5956696681664558131)
XLA Ops:
  10.6 25.4 %all-gather.6.cloned.1.call-done = f32[1,512,512]{2,0,1:T(1,128)} async-done(((f32[1,64,512]{2,0,1:T(1,128)}), f32[1,512,512]{2,0,1:T(1,128)}) %all-gather.6.cloned.1.call-update) | async-done | bytes 1048592 | tf_op jit(solution)/shard_map/all_gather | solution.py:54
  39.8 11.7 %cholesky.104 = f32[128,128]{1,0:T(8,128)S(1)} custom-call(f32[128,128]{1,0:T(8,128)S(1)} %cholesky.266), custom_call_target="Cholesky" | custom-call | tf_op jit(solution)/shard_map/jit(cholesky)/cholesky | solution.py:55
  51.6 9.8 %custom-call.31 = f32[1,128,128]{1,2,0:T(8,128)S(1)} custom-call(f32[1,128,128]{2,1,0:T(8,128)S(1)} %get-tuple-element.58), custom_call_target="InvertDiagBlocksLowerTriangular" | custom-call | tf_op jit(solution)/shard_map/jit(cholesky)/cholesky | solution.py:55
  62.2 11.7 %cholesky.217 = f32[128,128]{1,0:T(8,128)S(1)} custom-call(f32[128,128]{1,0:T(8,128)S(1)} %cholesky.270), custom_call_target="Cholesky" | custom-call | tf_op jit(solution)/shard_map/jit(cholesky)/cholesky | solution.py:55
  74.0 10.0 %custom-call.32 = f32[1,128,128]{1,2,0:T(8,128)S(1)} custom-call(f32[1,128,128]{2,1,0:T(8,128)S(1)} %get-tuple-element.55), custom_call_target="InvertDiagBlocksLowerTriangular" | custom-call | tf_op jit(solution)/shard_map/jit(cholesky)/cholesky | solution.py:55
  84.6 11.7 %cholesky.238 = f32[128,128]{1,0:T(8,128)S(1)} custom-call(f32[128,128]{1,0:T(8,128)S(1)} %cholesky.275), custom_call_target="Cholesky" | custom-call | tf_op jit(solution)/shard_map/jit(cholesky)/cholesky | solution.py:55
  97.1 9.8 %custom-call.33 = f32[1,128,128]{1,2,0:T(8,128)S(1)} custom-call(f32[1,128,128]{2,1,0:T(8,128)S(1)} %get-tuple-element.52), custom_call_target="InvertDiagBlocksLowerTriangular" | custom-call | tf_op jit(solution)/shard_map/jit(cholesky)/cholesky | solution.py:55
  107.5 11.7 %cholesky.255 = f32[128,128]{1,0:T(8,128)S(1)} custom-call(f32[128,128]{1,0:T(8,128)S(1)} %convolution_subtract_fusion.5), custom_call_target="Cholesky" | custom-call | tf_op jit(solution)/shard_map/jit(cholesky)/cholesky | solution.py:55
  124.3 10.4 %while.1 = (s32[]{:T(128)}, f32[512,512]{1,0:T(8,128)S(1)}, s32[4,2]{0,1:T(2,128)S(1)}, f32[4,128,128]{2,1,0:T(8,128)}, s32[]{:T(128)}) while((s32[]{:T(128)}, f32[512,512]{1,0:T(8,128)S(1)}, s32[4,2]{0,1:T(2,128)S(1)}, f32[4,128,128]{2,1,0:T(8,128)}, s32[]{:T(128)}) %tuple.46), condition=%wide.while_cond, body=%wide.while_body.sunk | while | flops 2 | bytes 132205 | solution.py:11
  134.8 40.6 %custom-call.34 = f32[4,128,128]{1,2,0:T(8,128)S(1)} custom-call(f32[4,128,128]{2,1,0:T(8,128)} %get-tuple-element.11), custom_call_target="InvertDiagBlocksLowerTriangular" | custom-call | tf_op jit(solution)/shard_map/jit(_solve_triangular)/triangular_solve | solution.py:11
  180.2 49.3 %all-gather.4.cloned.1.call-done = f32[4096,512]{0,1:T(8,128)} async-done(((f32[512,512]{0,1:T(8,128)}), f32[4096,512]{0,1:T(8,128)}) %all-gather.4.cloned.1.call-update) | async-done | bytes 8388624 | tf_op jit(solution)/shard_map/all_gather | solution.py:57
  229.5 16.5 %fusion.7 = f32[64,32,8,128]{3,2,1,0:T(8,128)S(1)} fusion(f32[1,512,4096]{2,1,0:T(8,128)} %param.8, f32[4096,512]{0,1:T(8,128)} %all-gather.4.cloned.1.call-done, f32[128,512]{1,0:T(8,128)S(1)} %fusion.33, f32[128,512]{1,0:T(8,128)S(1)} %fusion.34, f32[128,512]{1,0:T(8,128)S(1)} %fusion.36, f32[128,512]{1,0:T(8,128)S(1)} %fusion.21), kind=kOutput, calls=%fused_computation.16 | convolution fusion | flops 12887785472 | bytes 26214400 | tf_op jit(solution)/shard_map/dot_general | solution.py:59
  250.4 10.6 %gather_fusion.1 = f32[40,512,128]{2,1,0:T(8,128)} fusion(f32[512,32,128]{2,0,1:T(8,128)} %bitcast.114, s32[1024]{0:T(1024)S(1)} %pad_clamp_fusion), kind=kCustom, calls=%fused_computation.3 | custom fusion | bytes 20971680 | tf_op jit(solution)/shard_map/jit(_take)/gather | solution.py:63
  261.0 6.3 select_select_fusion.1
  267.3 122.3 %all_to_all.20 = f32[512,8,5,128]{3,0,2,1:T(8,128)} all-to-all(f32[512,8,5,128]{3,0,2,1:T(8,128)S(1)} %select_select_fusion.1), channel_id=1, replica_groups=mesh['front'=8,'row'=8,'col'=2] {'row'}, dimensions={1} | all-to-all | bytes 20971520 | tf_op jit(solution)/shard_map/all_to_all | solution.py:66
  389.6 9.2 %copy.46 = f32[8,512,1,5,128]{4,1,0,3,2:T(8,128)} copy(f32[8,512,1,5,128]{4,1,3,0,2:T(8,128)} %bitcast.116) | data formatting | bytes 20971520 | tf_op jit(solution)/shard_map/all_to_all | solution.py:66
  398.8 12.2 %gather_fusion.2 = f32[40,128,5,128]{3,1,2,0:T(8,128)} fusion(f32[32,128,5,128]{3,1,0,2:T(8,128)} %bitcast.112, s32[1024]{0:T(1024)S(1)} %pad_clamp_fusion), kind=kCustom, calls=%fused_computation.4 | custom fusion | bytes 26214560 | tf_op jit(solution)/shard_map/jit(_take)/gather | solution.py:70
  411.0 12.8 %select_select_fusion = f32[8,5,128,5,128]{4,2,3,1,0:T(8,128)} fusion(f32[8,5,128,5,128]{4,2,3,1,0:T(8,128)} %bitcast.113, pred[8,5]{1,0:T(8,128)(4,1)S(1)} %get-tuple-element.64, pred[8,5]{1,0:T(8,128)(4,1)S(1)} %get-tuple-element.63), kind=kLoop, calls=%fused_computation.12 | loop fusion | flops 6553600 | bytes 26214480 | tf_op jit(solution)/shard_map/jit(_where)/select_n | solution.py:72
  423.8 7.4 %all-to-all-start.1 = ((f32[8,5,128,5,128]{4,2,3,1,0:T(8,128)}), f32[8,5,128,5,128]{4,2,3,1,0:T(8,128)}, u32[]{:S(2)}, u32[]{:S(2)}) async-start(f32[8,5,128,5,128]{4,2,3,1,0:T(8,128)} %select_select_fusion), calls=%async_computation.1 | async-start | bytes 26214400 | tf_op jit(solution)/shard_map/all_to_all | solution.py:73
  437.3 187.8 %all-to-all-done.1 = f32[8,5,128,5,128]{4,2,3,1,0:T(8,128)} async-done(((f32[8,5,128,5,128]{4,2,3,1,0:T(8,128)}), f32[8,5,128,5,128]{4,2,3,1,0:T(8,128)}, u32[]{:S(2)}, u32[]{:S(2)}) %all-to-all-start.1) | async-done | bytes 13107232 | tf_op jit(solution)/shard_map/all_to_all | solution.py:73
  625.1 33.7 %fusion.4 = f32[8,5,128,12,128]{4,3,2,1,0:T(8,128)} fusion(f32[8,5,128,5,128]{4,2,3,1,0:T(8,128)} %all-to-all-done.1, s32[8,5]{1,0:T(8,128)S(1)} %select_subtract_fusion, pred[8,5]{1,0:T(8,128)(4,1)S(1)} %iota_compare_fusion.8), kind=kOutput, calls=%fused_computation.11 | convolution fusion | flops 471860160 | bytes 44564680 | tf_op jit(solution)/shard_map/fsxty,fbt->fsxby/dot_general | solution.py:78
  658.8 37.8 %fusion.8 = f32[12,128,12,128]{3,0,2,1:T(8,128)} fusion(f32[8,5,128,12,128]{4,3,2,1,0:T(8,128)} %fusion.4, s32[8,5]{0,1:T(8,128)S(1)} %copy.44, pred[8,5]{0,1:T(8,128)(4,1)S(1)} %iota_compare_fusion.9), kind=kOutput, calls=%fused_computation.17 | convolution fusion | flops 1132463104 | bytes 40894664 | tf_op jit(solution)/shard_map/fas,fsxby->axby/dot_general | solution.py:79
  696.6 12.4 %copy.49 = f32[12,128,12,128]{3,2,1,0:T(8,128)} copy(f32[12,128,12,128]{3,0,2,1:T(8,128)} %fusion.8) | data formatting | bytes 18874368 | tf_op jit(solution)/shard_map/fas,fsxby->axby/dot_general | solution.py:79
  709.0 11.9 %broadcast_in_dim_reshape.3 = f32[1,1536,1536]{2,1,0:T(8,128)} reshape(f32[12,128,12,128]{3,2,1,0:T(8,128)} %copy.49) | data formatting | bytes 18874368 | tf_op jit(solution)/shard_map/broadcast_in_dim;reshape | solution.py:82
  (79 shorter events, 38.3 us)
Async XLA Ops:
  7.2 28.8 %all-gather.6.cloned.1.call-start = ((), (), s32[]{:S(2)}) async-start(), calls=%async_computation.3 | async-start | bytes 1179648 | tf_op jit(solution)/shard_map/all_gather | solution.py:54
  8.9 220.6 %all-gather.4.cloned.1.call-start = ((), (), s32[]{:S(2)}) async-start(), calls=%async_computation.2 | async-start | bytes 9437184 | tf_op jit(solution)/shard_map/all_gather | solution.py:57
  38.4 141.4 %copy-start = (s32[16,32]{1,0:T(8,128)S(1)}, s32[16,32]{1,0:T(8,128)}, u32[]{:S(2)}) copy-start(s32[16,32]{1,0:T(8,128)} %param.9) | copy-start | bytes 6148
  423.8 201.3 %all-to-all-start.1 = ((f32[8,5,128,5,128]{4,2,3,1,0:T(8,128)}), f32[8,5,128,5,128]{4,2,3,1,0:T(8,128)}, u32[]{:S(2)}, u32[]{:S(2)}) async-start(f32[8,5,128,5,128]{4,2,3,1,0:T(8,128)} %select_select_fusion), calls=%async_computation.1 | async-start | bytes 26214400 | tf_op jit(solution)/shard_map/all_to_all | solution.py:73
Sparse Core Ops, SparseCore 0:
  10.3 25.6 all-gather.5
  179.9 49.5 all-gather.3
where the time goes:
time: 738 us; the launch traced here: 728 us
  waiting for transfers between devices  263 us (36%)
  other arithmetic  143 us (19%)
  blocking collectives  122 us (17%)
  matrix products  92.9 us (13%)
  local copies, waits for them, and re-layouts  82.6 us (11%)
  between operations  17.3 us (2%)
  starting transfers between devices  7.46 us (1%)
    all_to_all x1, waiting for transfers between devices, local(): lax.all_to_all(picked, 'front', split_axis=0, concat_axis=0, tiled=True)  188 us
    all_to_all x1, blocking collectives, local(): lax.all_to_all(source, 'row', split_axis=1, concat_axis=0, tiled=True)  122 us
    another operation x14, other arithmetic, local(): lower_factor = jnp.linalg.cholesky(pivot_whole)  78.6 us
    all_gather x1, waiting for transfers between devices, local(): all_factor = lax.all_gather(own_factor, 'row', axis=0, tiled=True)  49.3 us
    another operation x3, other arithmetic, solve_panel(): jax.scipy.linalg.solve_triangular(lower_factor, panel_block.T, lower=True)  41.8 us
    dot_general x1, matrix products, local(): jnp.einsum('fas,fsxby->axby', row_hot, partial_value, precision=lax.Preci...  37.8 us
    dot_general x1, matrix products, local(): jnp.einsum('fsxty,fbt->fsxby', routed, col_hot, precision=lax.Precision.H...  33.7 us
    all_gather x1, waiting for transfers between devices, local(): pivot_whole = lax.all_gather(pivot_block[0], 'row', axis=0, tiled=True)  25.4 us
  transfers between devices with their start and end apart: 3, of which 3 were waited for; matrix products, arithmetic and copies ran while one was open for 1% of the time, Pallas kernels for 0%

commit v1 on v0

--- a/solution.py
+++ b/solution.py
@@ -54,7 +54,12 @@
     pivot_whole = lax.all_gather(pivot_block[0], "row", axis=0, tiled=True)
     lower_factor = jnp.linalg.cholesky(pivot_whole)
     own_factor = solve_panel(lower_factor, panel_rows[0])
-    all_factor = lax.all_gather(own_factor, "row", axis=0, tiled=True)
+    ring = [own_factor]
+    for hop in range(7):
+        ring.append(lax.ppermute(ring[-1], "row", [(dev, (dev + 1) % 8) for dev in range(8)]))
+    all_factor = jnp.roll(
+        jnp.concatenate(ring[::-1], axis=0), (lax.axis_index("row") + 1) * ring[0].shape[0], axis=0
+    )
     col_picks, col_usable = block_slots(tile_ids, row_count, block_width, slot_count)
     contribution = update_block[0] - jnp.dot(
         own_factor, all_factor.T, precision=lax.Precision.HIGHEST

time: 738 us -> 828 us (1.12)
  waiting for transfers between devices: 263 us -> 321 us
  local copies, waits for them, and re-layouts: 82.6 us -> 112 us
    ppermute x0 -> x7, waiting for transfers between devices: none -> 108 us  [local(): lax.ppermute(ring[-1], 'row', [(dev, (dev + 1) % 8) for dev in range(8)])]
    all_gather x1 -> x0, waiting for transfers between devices: 49.3 us -> none  [local(): all_factor = lax.all_gather(own_factor, 'row', axis=0, tiled=True)]
    unnamed x5 -> x35, local copies, waits for them, and re-layouts: 4.57 us -> 33.8 us
  transfers between devices with their start and end apart: 3 -> 9, of which waited for: 3 -> 9; matrix products, arithmetic and copies ran while one was open for 1% -> 1% of each run, Pallas kernels for 0% -> 0%
where the time goes in v1:
time: 828 us; the launch traced here: 818 us
  waiting for transfers between devices  321 us (39%)
  other arithmetic  144 us (17%)
  blocking collectives  122 us (15%)
  local copies, waits for them, and re-layouts  112 us (14%)
  matrix products  93.7 us (11%)
  between operations  17.3 us (2%)
    all_to_all x1, waiting for transfers between devices, local(): lax.all_to_all(picked, 'front', split_axis=0, concat_axis=0, tiled=True)  188 us
    all_to_all x1, blocking collectives, local(): lax.all_to_all(source, 'row', split_axis=1, concat_axis=0, tiled=True)  122 us
    ppermute x7, waiting for transfers between devices, local(): lax.ppermute(ring[-1], 'row', [(dev, (dev + 1) % 8) for dev in range(8)])  108 us
    another operation x14, other arithmetic, local(): lower_factor = jnp.linalg.cholesky(pivot_whole)  78.6 us
    another operation x3, other arithmetic, solve_panel(): jax.scipy.linalg.solve_triangular(lower_factor, panel_block.T, lower=True)  41.7 us
    dot_general x1, matrix products, local(): jnp.einsum('fas,fsxby->axby', row_hot, partial_value, precision=lax.Preci...  37.8 us
    unnamed x35, local copies, waits for them, and re-layouts  33.8 us
    dot_general x1, matrix products, local(): jnp.einsum('fsxty,fbt->fsxby', routed, col_hot, precision=lax.Precision.H...  33.7 us
  transfers between devices with their start and end apart: 9, of which 9 were waited for; matrix products, arithmetic and copies ran while one was open for 1% of the time, Pallas kernels for 0%

profile of v1, /device:TPU:6, one launch (start us, length us, event | category | flops | bytes accessed | tf_op | source)
XLA Modules:
  0.0 818.2 jit_solution(8507095874185417128)
XLA Ops:
  10.5 25.5 %all-gather.3.cloned.1.call-done = f32[1,512,512]{2,0,1:T(1,128)} async-done(((f32[1,64,512]{2,0,1:T(1,128)}), f32[1,512,512]{2,0,1:T(1,128)}) %all-gather.3.cloned.1.call-update) | async-done | bytes 1048592 | tf_op jit(solution)/shard_map/all_gather | solution.py:54
  39.8 11.7 %cholesky.104 = f32[128,128]{1,0:T(8,128)S(1)} custom-call(f32[128,128]{1,0:T(8,128)S(1)} %cholesky.266), custom_call_target="Cholesky" | custom-call | tf_op jit(solution)/shard_map/jit(cholesky)/cholesky | solution.py:55
  62.2 11.7 %cholesky.217 = f32[128,128]{1,0:T(8,128)S(1)} custom-call(f32[128,128]{1,0:T(8,128)S(1)} %cholesky.270), custom_call_target="Cholesky" | custom-call | tf_op jit(solution)/shard_map/jit(cholesky)/cholesky | solution.py:55
  84.6 11.7 %cholesky.238 = f32[128,128]{1,0:T(8,128)S(1)} custom-call(f32[128,128]{1,0:T(8,128)S(1)} %cholesky.275), custom_call_target="Cholesky" | custom-call | tf_op jit(solution)/shard_map/jit(cholesky)/cholesky | solution.py:55
  107.5 11.7 %cholesky.255 = f32[128,128]{1,0:T(8,128)S(1)} custom-call(f32[128,128]{1,0:T(8,128)S(1)} %convolution_subtract_fusion.5), custom_call_target="Cholesky" | custom-call | tf_op jit(solution)/shard_map/jit(cholesky)/cholesky | solution.py:55
  124.3 10.4 %while.1 = (s32[]{:T(128)}, f32[512,512]{1,0:T(8,128)S(1)}, s32[4,2]{0,1:T(2,128)S(1)}, f32[4,128,128]{2,1,0:T(8,128)}, s32[]{:T(128)}) while((s32[]{:T(128)}, f32[512,512]{1,0:T(8,128)S(1)}, s32[4,2]{0,1:T(2,128)S(1)}, f32[4,128,128]{2,1,0:T(8,128)}, s32[]{:T(128)}) %tuple.46), condition=%wide.while_cond, body=%wide.while_body.sunk | while | flops 2 | bytes 132205 | solution.py:11
  134.7 40.5 %custom-call.34 = f32[4,128,128]{1,2,0:T(8,128)S(1)} custom-call(f32[4,128,128]{2,1,0:T(8,128)} %get-tuple-element.11), custom_call_target="InvertDiagBlocksLowerTriangular" | custom-call | tf_op jit(solution)/shard_map/jit(_solve_triangular)/triangular_solve | solution.py:11
  178.8 15.2 %collective-permute-done = f32[512,512]{0,1:T(8,128)S(1)} collective-permute-done((f32[512,512]{0,1:T(8,128)S(1)}, f32[512,512]{0,1:T(8,128)S(1)}, u32[]{:S(2)}, u32[]{:S(2)}) %collective-permute-start) | collective-permute-done | bytes 1048608 | tf_op jit(solution)/shard_map/ppermute | solution.py:59
  194.0 15.4 %collective-permute-done.1 = f32[512,512]{0,1:T(8,128)S(1)} collective-permute-done((f32[512,512]{0,1:T(8,128)S(1)}, f32[512,512]{0,1:T(8,128)S(1)}, u32[]{:S(2)}, u32[]{:S(2)}) %collective-permute-start.1) | collective-permute-done | bytes 1048608 | tf_op jit(solution)/shard_map/ppermute | solution.py:59
  210.4 15.4 %collective-permute-done.2 = f32[512,512]{0,1:T(8,128)S(1)} collective-permute-done((f32[512,512]{0,1:T(8,128)S(1)}, f32[512,512]{0,1:T(8,128)S(1)}, u32[]{:S(2)}, u32[]{:S(2)}) %collective-permute-start.2) | collective-permute-done | bytes 1048608 | tf_op jit(solution)/shard_map/ppermute | solution.py:59
  226.8 15.4 %collective-permute-done.3 = f32[512,512]{0,1:T(8,128)S(1)} collective-permute-done((f32[512,512]{0,1:T(8,128)S(1)}, f32[512,512]{0,1:T(8,128)S(1)}, u32[]{:S(2)}, u32[]{:S(2)}) %collective-permute-start.3) | collective-permute-done | bytes 1048608 | tf_op jit(solution)/shard_map/ppermute | solution.py:59
  243.2 15.5 %collective-permute-done.4 = f32[512,512]{0,1:T(8,128)} collective-permute-done((f32[512,512]{0,1:T(8,128)S(1)}, f32[512,512]{0,1:T(8,128)}, u32[]{:S(2)}, u32[]{:S(2)}) %collective-permute-start.4) | collective-permute-done | bytes 1048608 | tf_op jit(solution)/shard_map/ppermute | solution.py:59
  258.8 15.7 %collective-permute-done.5 = f32[512,512]{0,1:T(8,128)} collective-permute-done((f32[512,512]{0,1:T(8,128)}, f32[512,512]{0,1:T(8,128)}, u32[]{:S(2)}, u32[]{:S(2)}) %collective-permute-start.5) | collective-permute-done | bytes 1048608 | tf_op jit(solution)/shard_map/ppermute | solution.py:59
  275.0 15.3 %collective-permute-done.6 = f32[512,512]{0,1:T(8,128)} collective-permute-done((f32[512,512]{0,1:T(8,128)}, f32[512,512]{0,1:T(8,128)}, u32[]{:S(2)}, u32[]{:S(2)}) %collective-permute-start.6) | collective-permute-done | bytes 1048608 | tf_op jit(solution)/shard_map/ppermute | solution.py:59
  318.7 17.3 %fusion.7 = f32[64,32,8,128]{3,2,1,0:T(8,128)S(1)} fusion(f32[1,512,4096]{2,1,0:T(8,128)S(1)} %bitcast.121, f32[8192,512]{0,1:T(8,128)} %constant_dynamic-update-slice_fusion, s32[]{:T(128)S(6)} %select_n.110, f32[128,512]{1,0:T(8,128)S(1)} %fusion.37, f32[128,512]{1,0:T(8,128)S(1)} %fusion.38, f32[128,512]{1,0:T(8,128)S(1)} %fusion.40, ...), kind=kOutput, calls=%fused_computation.16 | convolution fusion | flops 12887785472 | bytes 26214404 | tf_op jit(solution)/shard_map/dot_general | solution.py:64
  340.4 10.5 %gather_fusion.1 = f32[40,512,128]{2,1,0:T(8,128)} fusion(f32[512,32,128]{2,0,1:T(8,128)} %bitcast.117, s32[1024]{0:T(1024)S(1)} %get-tuple-element.65), kind=kCustom, calls=%fused_computation.3 | custom fusion | bytes 20971680 | tf_op jit(solution)/shard_map/jit(_take)/gather | solution.py:68
  357.2 122.5 %all_to_all.20 = f32[512,8,5,128]{3,0,2,1:T(8,128)} all-to-all(f32[512,8,5,128]{3,0,2,1:T(8,128)S(1)} %select_select_fusion.1), channel_id=1, replica_groups=mesh['front'=8,'row'=8,'col'=2] {'row'}, dimensions={1} | all-to-all | bytes 20971520 | tf_op jit(solution)/shard_map/all_to_all | solution.py:71
  488.9 12.2 %gather_fusion.2 = f32[40,128,5,128]{3,1,2,0:T(8,128)} fusion(f32[32,128,5,128]{3,1,0,2:T(8,128)} %bitcast.115, s32[1024]{0:T(1024)S(1)} %get-tuple-element.65), kind=kCustom, calls=%fused_computation.4 | custom fusion | bytes 26214560 | tf_op jit(solution)/shard_map/jit(_take)/gather | solution.py:75
  501.1 12.8 %select_select_fusion = f32[8,5,128,5,128]{4,2,3,1,0:T(8,128)} fusion(f32[8,5,128,5,128]{4,2,3,1,0:T(8,128)} %bitcast.116, pred[8,5]{1,0:T(8,128)(4,1)S(1)} %get-tuple-element.64, pred[8,5]{1,0:T(8,128)(4,1)S(1)} %get-tuple-element.63), kind=kLoop, calls=%fused_computation.12 | loop fusion | flops 6553600 | bytes 26214480 | tf_op jit(solution)/shard_map/jit(_where)/select_n | solution.py:77
  527.5 187.7 %all-to-all-done.1 = f32[8,5,128,5,128]{4,2,3,1,0:T(8,128)} async-done(((f32[8,5,128,5,128]{4,2,3,1,0:T(8,128)}), f32[8,5,128,5,128]{4,2,3,1,0:T(8,128)}, u32[]{:S(2)}, u32[]{:S(2)}) %all-to-all-start.1) | async-done | bytes 13107232 | tf_op jit(solution)/shard_map/all_to_all | solution.py:78
  715.2 33.7 %fusion.4 = f32[8,5,128,12,128]{4,3,2,1,0:T(8,128)} fusion(f32[8,5,128,5,128]{4,2,3,1,0:T(8,128)} %all-to-all-done.1, s32[8,5]{1,0:T(8,128)S(1)} %select_subtract_fusion, pred[8,5]{1,0:T(8,128)(4,1)S(1)} %iota_compare_fusion.8), kind=kOutput, calls=%fused_computation.11 | convolution fusion | flops 471860160 | bytes 44564680 | tf_op jit(solution)/shard_map/fsxty,fbt->fsxby/dot_general | solution.py:83
  748.8 37.8 %fusion.10 = f32[12,128,12,128]{3,0,2,1:T(8,128)} fusion(f32[8,5,128,12,128]{4,3,2,1,0:T(8,128)} %fusion.4, s32[8,5]{0,1:T(8,128)S(1)} %copy.44, pred[8,5]{0,1:T(8,128)(4,1)S(1)} %iota_compare_fusion.9), kind=kOutput, calls=%fused_computation.19 | convolution fusion | flops 1132463104 | bytes 40894664 | tf_op jit(solution)/shard_map/fas,fsxby->axby/dot_general | solution.py:84
  786.7 12.4 %copy.49 = f32[12,128,12,128]{3,2,1,0:T(8,128)} copy(f32[12,128,12,128]{3,0,2,1:T(8,128)} %fusion.10) | data formatting | bytes 18874368 | tf_op jit(solution)/shard_map/fas,fsxby->axby/dot_general | solution.py:84
  799.1 11.9 %broadcast_in_dim_reshape.3 = f32[1,1536,1536]{2,1,0:T(8,128)} reshape(f32[12,128,12,128]{3,2,1,0:T(8,128)} %copy.49) | data formatting | bytes 18874368 | tf_op jit(solution)/shard_map/broadcast_in_dim;reshape | solution.py:87
  (123 shorter events, 121.3 us)
Async XLA Ops:
  7.2 267.4 %copy-start.6 = (s32[16,32]{1,0:T(8,128)S(1)}, s32[16,32]{1,0:T(8,128)}, u32[]{:S(2)}) copy-start(s32[16,32]{1,0:T(8,128)} %param.9) | copy-start | bytes 6148
  7.2 28.8 %all-gather.3.cloned.1.call-start = ((), (), s32[]{:S(2)}) async-start(), calls=%async_computation.2 | async-start | bytes 1179648 | tf_op jit(solution)/shard_map/all_gather | solution.py:54
  178.5 15.4 %collective-permute-start = (f32[512,512]{0,1:T(8,128)S(1)}, f32[512,512]{0,1:T(8,128)S(1)}, u32[]{:S(2)}, u32[]{:S(2)}) collective-permute-start(f32[512,512]{0,1:T(8,128)S(1)} %get-tuple-element.47), channel_id=1, source_target_pairs={{0,2},{2,4},{4,6},{6,8},{8,10},{10,12},{12,14},{14,0},{1,3},{3,5},... | collective-permute-start | bytes 3145736 | tf_op jit(solution)/shard_map/ppermute | solution.py:59
  194.0 15.4 %collective-permute-start.1 = (f32[512,512]{0,1:T(8,128)S(1)}, f32[512,512]{0,1:T(8,128)S(1)}, u32[]{:S(2)}, u32[]{:S(2)}) collective-permute-start(f32[512,512]{0,1:T(8,128)S(1)} %collective-permute-done), channel_id=1, source_target_pairs={{0,2},{2,4},{4,6},{6,8},{8,10},{10,12},{12,14},{14,0},{1,3},{3,5},... | collective-permute-start | bytes 3145736 | tf_op jit(solution)/shard_map/ppermute | solution.py:59
  209.4 1.0 copy-start
  210.4 15.4 %collective-permute-start.2 = (f32[512,512]{0,1:T(8,128)S(1)}, f32[512,512]{0,1:T(8,128)S(1)}, u32[]{:S(2)}, u32[]{:S(2)}) collective-permute-start(f32[512,512]{0,1:T(8,128)S(1)} %collective-permute-done.1), channel_id=1, source_target_pairs={{0,2},{2,4},{4,6},{6,8},{8,10},{10,12},{12,14},{14,0},{1,3},{3,5},... | collective-permute-start | bytes 3145736 | tf_op jit(solution)/shard_map/ppermute | solution.py:59
  225.9 1.0 copy-start.2
  226.8 15.4 %collective-permute-start.3 = (f32[512,512]{0,1:T(8,128)S(1)}, f32[512,512]{0,1:T(8,128)S(1)}, u32[]{:S(2)}, u32[]{:S(2)}) collective-permute-start(f32[512,512]{0,1:T(8,128)S(1)} %collective-permute-done.2), channel_id=1, source_target_pairs={{0,2},{2,4},{4,6},{6,8},{8,10},{10,12},{12,14},{14,0},{1,3},{3,5},... | collective-permute-start | bytes 3145736 | tf_op jit(solution)/shard_map/ppermute | solution.py:59
  242.3 1.0 copy-start.4
  243.2 15.5 %collective-permute-start.4 = (f32[512,512]{0,1:T(8,128)S(1)}, f32[512,512]{0,1:T(8,128)}, u32[]{:S(2)}, u32[]{:S(2)}) collective-permute-start(f32[512,512]{0,1:T(8,128)S(1)} %collective-permute-done.3), channel_id=1, source_target_pairs={{0,2},{2,4},{4,6},{6,8},{8,10},{10,12},{12,14},{14,0},{1,3},{3,5},... | collective-permute-start | bytes 3145736 | tf_op jit(solution)/shard_map/ppermute | solution.py:59
  258.8 15.8 %collective-permute-start.5 = (f32[512,512]{0,1:T(8,128)}, f32[512,512]{0,1:T(8,128)}, u32[]{:S(2)}, u32[]{:S(2)}) collective-permute-start(f32[512,512]{0,1:T(8,128)} %collective-permute-done.4), channel_id=1, source_target_pairs={{0,2},{2,4},{4,6},{6,8},{8,10},{10,12},{12,14},{14,0},{1,3},{3,5},... | collective-permute-start | bytes 3145736 | tf_op jit(solution)/shard_map/ppermute | solution.py:59
  274.5 15.8 %collective-permute-start.6 = (f32[512,512]{0,1:T(8,128)}, f32[512,512]{0,1:T(8,128)}, u32[]{:S(2)}, u32[]{:S(2)}) collective-permute-start(f32[512,512]{0,1:T(8,128)} %collective-permute-done.5), channel_id=1, source_target_pairs={{0,2},{2,4},{4,6},{6,8},{8,10},{10,12},{12,14},{14,0},{1,3},{3,5},... | collective-permute-start | bytes 3145736 | tf_op jit(solution)/shard_map/ppermute | solution.py:59
  274.9 38.6 %copy-start.5 = (f32[512,512]{0,1:T(8,128)S(1)}, f32[512,512]{0,1:T(8,128)}, u32[]{:S(2)}) copy-start(f32[512,512]{0,1:T(8,128)} %copy-done.4) | copy-start | bytes 3145732
  274.9 39.6 %copy-start.3 = (f32[512,512]{0,1:T(8,128)S(1)}, f32[512,512]{0,1:T(8,128)}, u32[]{:S(2)}) copy-start(f32[512,512]{0,1:T(8,128)} %copy-done.2) | copy-start | bytes 3145732
  274.9 40.7 %copy-start.1 = (f32[512,512]{0,1:T(8,128)S(1)}, f32[512,512]{0,1:T(8,128)}, u32[]{:S(2)}) copy-start(f32[512,512]{0,1:T(8,128)} %copy-done) | copy-start | bytes 3145732
  275.0 43.7 %slice-start = ((s8[8388608]{0:T(1024)(128)(4,1)}), s8[4194304]{0:T(1024)(128)(4,1)S(1)}, s32[]{:S(2)}) async-start(s8[8388608]{0:T(1024)(128)(4,1)} %bitcast.120), calls=%async_computation.3 | async-start | bytes 8388608
  305.0 13.7 %slice-start.1 = ((s8[8388608]{0:T(1024)(128)(4,1)}), s8[4194304]{0:T(1024)(128)(4,1)S(1)}, s32[]{:S(2)}) async-start(s8[8388608]{0:T(1024)(128)(4,1)} %bitcast.120), calls=%async_computation.4 | async-start | bytes 8388608
  513.9 201.3 %all-to-all-start.1 = ((f32[8,5,128,5,128]{4,2,3,1,0:T(8,128)}), f32[8,5,128,5,128]{4,2,3,1,0:T(8,128)}, u32[]{:S(2)}, u32[]{:S(2)}) async-start(f32[8,5,128,5,128]{4,2,3,1,0:T(8,128)} %select_select_fusion), calls=%async_computation.1 | async-start | bytes 26214400 | tf_op jit(solution)/shard_map/all_to_all | solution.py:78
Sparse Core Ops, SparseCore 0:
  10.3 25.6 all-gather.2
